TPU v7x, 32 devices: a whole 2x2x4 slice. The times are simulated.
32 devices in a mesh: rep: 2 (over x), fsdp: 16 (over z, y, core).
Axes of the slice: x: 2, y: 2, z: 4, core: 2. Of those that a mesh axis runs over, the one named last changes fastest.
Arguments:
- tokens_in: bfloat16 [37632, 768], P(('rep', 'fsdp')), may hold values from -6 to 6
- token_image: int32 [37632], P(('rep', 'fsdp')), may hold values from 0 to 5, as said below
- joined_weight: bfloat16 [768, 5376], P('fsdp'), may hold values from -0.21875 to 0.21875
- heads_weight: bfloat16 [768, 768], P('fsdp'), may hold values from -1.75 to 1.75
- down_weight: bfloat16 [3072, 768], P('fsdp'), may hold values from -0.109375 to 0.109375
- norm_gain: bfloat16 [768], P('fsdp'), may hold values from 0.25 to 1.75
- query_gain: bfloat16 [64], P('fsdp'), may hold values from 0.25 to 1.75
- key_gain: bfloat16 [64], P('fsdp'), may hold values from 0.25 to 1.75
- hidden_bias: bfloat16 [3072], P('fsdp'), may hold values from -3 to 3
- output_bias: bfloat16 [768], P('fsdp'), may hold values from -3 to 3
- cotangent: bfloat16 [37632, 768], P(('rep', 'fsdp')), may hold values from -6 to 6
Outputs:
- block_out: bfloat16 [37632, 768], P(('rep', 'fsdp'))
- grad_tokens: bfloat16 [37632, 768], P(('rep', 'fsdp'))
- grad_joined: float32 [768, 5376], P('fsdp')
- grad_heads: float32 [768, 768], P('fsdp')
- grad_down: float32 [3072, 768], P('fsdp')
- grad_norm: float32 [768], P('fsdp')
- grad_query: float32 [64], P('fsdp')
- grad_key: float32 [64], P('fsdp')
- grad_hidden: float32 [3072], P('fsdp')
- grad_output: float32 [768], P('fsdp')
Inputs may be any that keep to these rules, and one draw needn't show every extreme that they name: `token_image`: in each aligned block of 1176 tokens (the tokens of one device) either all tokens are 0 (one image), or token t of the block is t // 196 (6 images of 196 consecutive tokens). In every draw some block holds one image and some block holds 6.
All inputs are finite; a program needn't handle non-finite values.
Results may differ from a plain program's by a relative error of at most 0.013.
Values may be sent and summed in bfloat16 or wider, within the bound.
No kernel may reach another device: no remote copies, remote signals or barrier semaphores. Data moves between devices by JAX's collectives and lax.ppermute only.
A program may use at most 320 MiB of HBM per device.

v0:
```python
from functools import partial

import jax
import jax.numpy as jnp
from jax import lax
from jax.sharding import PartitionSpec as P

SHORT = 196


norm_eps = 1e-06


def layer_norm(values, gain_row):
    row_mean = jnp.mean(values, axis=-1, keepdims=True)
    centered = values - row_mean
    variance = jnp.mean(centered * centered, axis=-1, keepdims=True)
    return centered * lax.rsqrt(variance + norm_eps) * gain_row


def head_norm(pre_rows, gain_row):
    length = pre_rows.shape[0]
    shaped = pre_rows.reshape(length, -1, gain_row.shape[0])
    return layer_norm(shaped, gain_row).reshape(length, -1)


def gelu_exact(values):
    return jax.nn.gelu(values, approximate=False)


def to_pairs(rows_in, pair_width):
    length = rows_in.shape[0]
    return rows_in.reshape(length, -1, pair_width).transpose(1, 0, 2)


def from_pairs(stacked):
    return stacked.transpose(1, 0, 2).reshape(stacked.shape[1], -1)


def pair_forward(single_image, pieces):
    query_rows, key_rows, value_rows = pieces
    length = query_rows.shape[0]
    head_size = query_rows.shape[1] // 2
    scale = head_size ** (-0.5)

    def long_path(operands):
        query_all, key_all, value_all = (
            operand_part.reshape(length, 2, head_size) for operand_part in operands
        )
        scores = (
            jnp.einsum("qhd,khd->hqk", query_all, key_all, preferred_element_type=jnp.float32)
            * scale
        )
        row_max = jnp.max(scores, axis=-1, keepdims=True)
        row_total = jnp.sum(jnp.exp(scores - row_max), axis=-1, keepdims=True)
        logsum = row_max + jnp.log(row_total)
        probs_low = jnp.exp(scores - logsum).astype(jnp.bfloat16)
        mixed_rows = jnp.einsum(
            "hqk,khd->qhd", probs_low, value_all, preferred_element_type=jnp.float32
        )
        return (mixed_rows.reshape(length, -1), logsum[:, :, 0])

    def short_path(operands):
        images = length // SHORT
        query_all, key_all, value_all = (
            operand_part.reshape(images, SHORT, 2, head_size) for operand_part in operands
        )
        scores = (
            jnp.einsum("bqhd,bkhd->bhqk", query_all, key_all, preferred_element_type=jnp.float32)
            * scale
        )
        row_max = jnp.max(scores, axis=-1, keepdims=True)
        row_total = jnp.sum(jnp.exp(scores - row_max), axis=-1, keepdims=True)
        logsum = row_max + jnp.log(row_total)
        probs_low = jnp.exp(scores - logsum).astype(jnp.bfloat16)
        mixed_rows = jnp.einsum(
            "bhqk,bkhd->bqhd", probs_low, value_all, preferred_element_type=jnp.float32
        )
        return (
            mixed_rows.reshape(length, -1),
            logsum[..., 0].transpose(1, 0, 2).reshape(2, length),
        )

    return lax.cond(single_image, long_path, short_path, (query_rows, key_rows, value_rows))


def pair_backward(single_image, pieces):
    query_rows, key_rows, value_rows, grad_low, logsum = pieces
    length = query_rows.shape[0]
    head_size = query_rows.shape[1] // 2
    scale = head_size ** (-0.5)

    def long_path(operands):
        query_all, key_all, value_all, grad_all = (
            operand_part.reshape(length, 2, head_size) for operand_part in operands[:4]
        )
        logsum_all = operands[4]
        scores = (
            jnp.einsum("qhd,khd->hqk", query_all, key_all, preferred_element_type=jnp.float32)
            * scale
        )
        probs = jnp.exp(scores - logsum_all[:, :, None])
        probs_low = probs.astype(jnp.bfloat16)
        grad_probs = jnp.einsum(
            "qhd,khd->hqk", grad_all, value_all, preferred_element_type=jnp.float32
        )
        row_delta = jnp.sum(probs * grad_probs, axis=-1, keepdims=True)
        grad_scores = (probs * (grad_probs - row_delta)).astype(jnp.bfloat16)
        grad_query = (
            jnp.einsum("hqk,khd->qhd", grad_scores, key_all, preferred_element_type=jnp.float32)
            * scale
        )
        grad_key = (
            jnp.einsum("hqk,qhd->khd", grad_scores, query_all, preferred_element_type=jnp.float32)
            * scale
        )
        grad_value = jnp.einsum(
            "hqk,qhd->khd", probs_low, grad_all, preferred_element_type=jnp.float32
        )
        return tuple(
            (grad_part.reshape(length, -1) for grad_part in (grad_query, grad_key, grad_value))
        )

    def short_path(operands):
        images = length // SHORT
        query_all, key_all, value_all, grad_all = (
            operand_part.reshape(images, SHORT, 2, head_size) for operand_part in operands[:4]
        )
        logsum_all = operands[4].reshape(2, images, SHORT).transpose(1, 0, 2)
        scores = (
            jnp.einsum("bqhd,bkhd->bhqk", query_all, key_all, preferred_element_type=jnp.float32)
            * scale
        )
        probs = jnp.exp(scores - logsum_all[..., None])
        probs_low = probs.astype(jnp.bfloat16)
        grad_probs = jnp.einsum(
            "bqhd,bkhd->bhqk", grad_all, value_all, preferred_element_type=jnp.float32
        )
        row_delta = jnp.sum(probs * grad_probs, axis=-1, keepdims=True)
        grad_scores = (probs * (grad_probs - row_delta)).astype(jnp.bfloat16)
        grad_query = (
            jnp.einsum("bhqk,bkhd->bqhd", grad_scores, key_all, preferred_element_type=jnp.float32)
            * scale
        )
        grad_key = (
            jnp.einsum(
                "bhqk,bqhd->bkhd", grad_scores, query_all, preferred_element_type=jnp.float32
            )
            * scale
        )
        grad_value = jnp.einsum(
            "bhqk,bqhd->bkhd", probs_low, grad_all, preferred_element_type=jnp.float32
        )
        return tuple(
            (grad_part.reshape(length, -1) for grad_part in (grad_query, grad_key, grad_value))
        )

    return lax.cond(
        single_image, long_path, short_path, (query_rows, key_rows, value_rows, grad_low, logsum)
    )


def per_device(
    tokens_in,
    token_image,
    joined_weight,
    heads_weight,
    down_weight,
    norm_gain,
    query_gain,
    key_gain,
    hidden_bias,
    output_bias,
    cotangent,
):
    (
        joined_full,
        heads_full,
        down_full,
        norm_full,
        query_full,
        key_full,
        bias_hidden,
        bias_output,
    ) = (
        lax.all_gather(joined_weight, "fsdp", axis=0, tiled=True),
        lax.all_gather(heads_weight, "fsdp", axis=0, tiled=True),
        lax.all_gather(down_weight, "fsdp", axis=0, tiled=True),
        lax.all_gather(norm_gain, "fsdp", axis=0, tiled=True),
        lax.all_gather(query_gain, "fsdp", axis=0, tiled=True),
        lax.all_gather(key_gain, "fsdp", axis=0, tiled=True),
        lax.all_gather(hidden_bias, "fsdp", axis=0, tiled=True),
        lax.all_gather(output_bias, "fsdp", axis=0, tiled=True),
    )
    width = norm_full.shape[0]
    pair_width = 2 * query_full.shape[0]
    single_image = token_image[0] == token_image[-1]
    token_rows = tokens_in.astype(jnp.float32)
    normed_low = layer_norm(token_rows, norm_full.astype(jnp.float32)).astype(jnp.bfloat16)
    projected = jnp.dot(normed_low, joined_full, preferred_element_type=jnp.float32)
    query_low = head_norm(projected[:, :width], query_full.astype(jnp.float32)).astype(jnp.bfloat16)
    key_low = head_norm(projected[:, width : 2 * width], key_full.astype(jnp.float32)).astype(
        jnp.bfloat16
    )
    value_low = projected[:, 2 * width : 3 * width].astype(jnp.bfloat16)
    inner_sum = projected[:, 3 * width :] + bias_hidden.astype(jnp.float32)
    activ_full, gelu_back = jax.vjp(gelu_exact, inner_sum)
    activated = activ_full.astype(jnp.bfloat16)
    query_pairs = to_pairs(query_low, pair_width)
    key_pairs = to_pairs(key_low, pair_width)
    value_pairs = to_pairs(value_low, pair_width)
    mixed_pairs, logsum_pairs = lax.map(
        partial(pair_forward, single_image), (query_pairs, key_pairs, value_pairs)
    )
    mixed_low = from_pairs(mixed_pairs).astype(jnp.bfloat16)
    block_sum = token_rows + jnp.dot(mixed_low, heads_full, preferred_element_type=jnp.float32)
    block_sum = (
        block_sum
        + jnp.dot(activated, down_full, preferred_element_type=jnp.float32)
        + bias_output.astype(jnp.float32)
    )
    block_out = block_sum.astype(jnp.bfloat16)
    joined_back, heads_back, down_back, norm_again, query_again, key_again = (
        lax.all_gather(joined_weight, "fsdp", axis=0, tiled=True),
        lax.all_gather(heads_weight, "fsdp", axis=0, tiled=True),
        lax.all_gather(down_weight, "fsdp", axis=0, tiled=True),
        lax.all_gather(norm_gain, "fsdp", axis=0, tiled=True),
        lax.all_gather(query_gain, "fsdp", axis=0, tiled=True),
        lax.all_gather(key_gain, "fsdp", axis=0, tiled=True),
    )
    cot_rows = cotangent.astype(jnp.float32)
    grad_down = jnp.dot(activated.T, cotangent, preferred_element_type=jnp.float32)
    grad_heads = jnp.dot(mixed_low.T, cotangent, preferred_element_type=jnp.float32)
    grad_output = jnp.sum(cot_rows, axis=0)
    grad_activ = jnp.dot(cotangent, down_back.T, preferred_element_type=jnp.float32)
    grad_inner = gelu_back(grad_activ)[0]
    grad_hidden = jnp.sum(grad_inner, axis=0)
    grad_mixed = jnp.dot(cotangent, heads_back.T, preferred_element_type=jnp.float32).astype(
        jnp.bfloat16
    )
    grad_qn_pairs, grad_kn_pairs, grad_v_pairs = lax.map(
        partial(pair_backward, single_image),
        (query_pairs, key_pairs, value_pairs, to_pairs(grad_mixed, pair_width), logsum_pairs),
    )
    _, query_back = jax.vjp(head_norm, projected[:, :width], query_again.astype(jnp.float32))
    grad_qpre, grad_query = query_back(from_pairs(grad_qn_pairs))
    _, key_back = jax.vjp(head_norm, projected[:, width : 2 * width], key_again.astype(jnp.float32))
    grad_kpre, grad_key = key_back(from_pairs(grad_kn_pairs))
    grad_proj = jnp.concatenate(
        (grad_qpre, grad_kpre, from_pairs(grad_v_pairs), grad_inner), axis=1
    ).astype(jnp.bfloat16)
    grad_joined = jnp.dot(normed_low.T, grad_proj, preferred_element_type=jnp.float32)
    grad_normed = jnp.dot(grad_proj, joined_back.T, preferred_element_type=jnp.float32)
    _, norm_back = jax.vjp(layer_norm, token_rows, norm_again.astype(jnp.float32))
    grad_from_norm, grad_norm = norm_back(grad_normed)
    grad_tokens = (cot_rows + grad_from_norm).astype(jnp.bfloat16)
    (
        shard_joined,
        shard_heads,
        shard_down,
        shard_norm,
        shard_query,
        shard_key,
        shard_hidden,
        shard_output,
    ) = (
        lax.psum_scatter(grad_joined, "fsdp", scatter_dimension=0, tiled=True),
        lax.psum_scatter(grad_heads, "fsdp", scatter_dimension=0, tiled=True),
        lax.psum_scatter(grad_down, "fsdp", scatter_dimension=0, tiled=True),
        lax.psum_scatter(grad_norm, "fsdp", scatter_dimension=0, tiled=True),
        lax.psum_scatter(grad_query, "fsdp", scatter_dimension=0, tiled=True),
        lax.psum_scatter(grad_key, "fsdp", scatter_dimension=0, tiled=True),
        lax.psum_scatter(grad_hidden, "fsdp", scatter_dimension=0, tiled=True),
        lax.psum_scatter(grad_output, "fsdp", scatter_dimension=0, tiled=True),
    )
    (
        total_joined,
        total_heads,
        total_down,
        total_norm,
        total_query,
        total_key,
        total_hidden,
        total_output,
    ) = (
        lax.psum(shard_joined.astype(jnp.bfloat16), "rep").astype(jnp.float32),
        lax.psum(shard_heads.astype(jnp.bfloat16), "rep").astype(jnp.float32),
        lax.psum(shard_down.astype(jnp.bfloat16), "rep").astype(jnp.float32),
        lax.psum(shard_norm.astype(jnp.bfloat16), "rep").astype(jnp.float32),
        lax.psum(shard_query.astype(jnp.bfloat16), "rep").astype(jnp.float32),
        lax.psum(shard_key.astype(jnp.bfloat16), "rep").astype(jnp.float32),
        lax.psum(shard_hidden.astype(jnp.bfloat16), "rep").astype(jnp.float32),
        lax.psum(shard_output.astype(jnp.bfloat16), "rep").astype(jnp.float32),
    )
    return (
        block_out,
        grad_tokens,
        total_joined,
        total_heads,
        total_down,
        total_norm,
        total_query,
        total_key,
        total_hidden,
        total_output,
    )


def solution(mesh):
    return jax.shard_map(
        per_device,
        mesh=mesh,
        in_specs=(
            P(("rep", "fsdp"), None),
            P(("rep", "fsdp")),
            P("fsdp", None),
            P("fsdp", None),
            P("fsdp", None),
            P("fsdp"),
            P("fsdp"),
            P("fsdp"),
            P("fsdp"),
            P("fsdp"),
            P(("rep", "fsdp"), None),
        ),
        out_specs=(
            P(("rep", "fsdp"), None),
            P(("rep", "fsdp"), None),
            P("fsdp", None),
            P("fsdp", None),
            P("fsdp", None),
            P("fsdp"),
            P("fsdp"),
            P("fsdp"),
            P("fsdp"),
            P("fsdp"),
        ),
        check_vma=False,
    )
```

profile of v0, /device:TPU:0, one launch (start us, length us, event | category | flops | bytes accessed | tf_op | source)
XLA Modules:
  0.0 931.2 jit_solution(9466872848657195147)
XLA Ops:
  18.4 64.4 %all-reduce.11 = (bf16[768]{0:T(1024)(128)(2,1)S(1)}, bf16[64]{0:T(256)(128)(2,1)S(1)}, bf16[64]{0:T(256)(128)(2,1)S(1)}, bf16[3072]{0:T(1024)(128)(2,1)S(1)}, bf16[768]{0:T(1024)(128)(2,1)}) all-reduce(bf16[768]{0:T(1024)(128)(2,1)S(1)} %dynamic-update-slice, ...), channel_id=1, replica_groups=mesh['rep'=2,'fsdp'=16] {'fsdp'}, use_global_device_ids=true, to_apply=%add | all-reduce | flops 4736 | bytes 18944
  100.0 26.3 %all-gather.4.cloned.1.call-done = bf16[768,5376]{1,0:T(8,128)(2,1)} async-done(((bf16[48,5376]{1,0:T(8,128)(2,1)}), bf16[768,5376]{1,0:T(8,128)(2,1)}) %all-gather.4.cloned.1.call-update) | async-done | bytes 8257552 | tf_op jit(solution)/shard_map/all_gather | solution.py:186
  126.3 17.5 %fusion.61 = f32[1176,5376]{1,0:T(8,128)} fusion(bf16[768,5376]{1,0:T(8,128)(2,1)} %all-gather.4.cloned.1.call-done, bf16[1176,768]{1,0:T(8,128)(2,1)S(1)} %copy-done.13, f32[768]{0:T(1024)S(1)} %convert_element_type.129, f32[1176]{0:T(1024)S(1)} %fusion.57, f32[1176]{0:T(1024)S(1)} %broadcast_multiply_fusion.2), kind=kOutput, calls=%fused_computation.148 | convolution fusion | flops 9715378176 | bytes 35365056 | tf_op jit(solution)/shard_map/dot_general | solution.py:200
  143.8 6.7 fusion.66
  201.2 5.6 copy.188
  206.8 10.0 %multiply_convert_fusion.3 = (bf16[1176,768]{1,0:T(8,128)(2,1)S(1)}, bf16[1176,768]{1,0:T(8,128)(2,1)}) fusion(f32[1176,768]{1,0:T(8,128)} %copy.189, f32[768]{0:T(1024)S(1)} %mul.323, f32[1176,768]{1,0:T(8,128)} %copy.188, f32[1176,5376]{1,0:T(8,128)} %fusion.61, f32[768]{0:T(1024)S(1)} %mul.315, f32[1176,768]{1,0:T(8,128)} %copy.185, f32[1176,768]{1,0:T(8,128)} %copy.184), kind=kLoop, calls=%fused_computation.118 | loop fusion | flops 7225344 | bytes 25294848 | tf_op jit(solution)/shard_map/convert_element_type | solution.py:202
  227.0 70.7 %while.28 = (s32[]{:T(128)}, bf16[6,1176,128]{1,2,0:T(8,128)(2,1)}, f32[6,2,1176]{2,1,0:T(2,128)}, pred[]{:T(512)}, bf16[6,1176,128]{1,2,0:T(8,128)(2,1)}, /*ind...) while((s32[]{:T(128)}, bf16[6,1176,128]{1,2,0:T(8,128)(2,1)}, ...), condition=%wide.region_13.14_spmd.clone, body=%wide.region_6.13_spmd.sunk.clone | while | flops 724677056 | bytes 36918208 | solution.py:212
  229.1 7.6 conditional.6
  240.9 7.6 conditional.6
  252.7 7.6 conditional.6
  264.5 7.6 conditional.6
  276.3 7.6 conditional.6
  288.0 7.6 conditional.6
  302.9 34.3 %multiply_convert_fusion.2 = (bf16[1176,3072]{1,0:T(8,128)(2,1)S(1)}, f32[1176,3072]{1,0:T(8,128)}) fusion(f32[1176,5376]{1,0:T(8,128)} %fusion.61, f32[3072]{0:T(1024)S(1)} %convert_element_type.138), kind=kLoop, calls=%fused_computation.61 | loop fusion | flops 238436352 | bytes 36139008 | tf_op jit(solution)/shard_map/convert_element_type | solution.py:208
  340.2 9.1 fusion.73
  349.4 168.0 %while.29 = (s32[]{:T(128)}, f32[6,1176,128]{1,2,0:T(8,128)}, f32[6,1176,128]{1,2,0:T(8,128)}, bf16[6,1176,128]{1,2,0:T(8,128)(2,1)}, pred[]{:T(512)}, /*index=5...) while((s32[]{:T(128)}, f32[6,1176,128]{1,2,0:T(8,128)}, ...), condition=%wide.region_19.20_spmd.clone, body=%wide.region_14.19_spmd.sunk.clone | while | flops 1792635520 | bytes 92298616 | solution.py:241
  362.1 18.8 %conditional.7 = (f32[1,1176,128]{1,2,0:T(8,128)}, f32[1,1176,128]{1,2,0:T(8,128)}, bf16[1,1176,128]{1,2,0:T(8,128)(2,1)S(1)}) conditional(s32[]{:T(128)} %convert_element_type.225, (bf16[1176,128]{0,1:T(8,128)(2,1)S(1)}, bf16[1176,128]{0,1:T(8,128)(2,1)S(1)}, f32[2,1176]{1,0:T(2,128)S(1)}, bf16[1176,128]{0,1:T(8,128)(2,1)S(1)}, ...), branch_computations={%region_15.16_spmd, %region_17.18_spmd} | conditional | flops 1792635520 | bytes 86619480 | solution.py:158
  388.9 18.5 %conditional.7 = (f32[1,1176,128]{1,2,0:T(8,128)}, f32[1,1176,128]{1,2,0:T(8,128)}, bf16[1,1176,128]{1,2,0:T(8,128)(2,1)S(1)}) conditional(s32[]{:T(128)} %convert_element_type.225, (bf16[1176,128]{0,1:T(8,128)(2,1)S(1)}, bf16[1176,128]{0,1:T(8,128)(2,1)S(1)}, f32[2,1176]{1,0:T(2,128)S(1)}, bf16[1176,128]{0,1:T(8,128)(2,1)S(1)}, ...), branch_computations={%region_15.16_spmd, %region_17.18_spmd} | conditional | flops 1792635520 | bytes 86619480 | solution.py:158
  415.1 18.5 %conditional.7 = (f32[1,1176,128]{1,2,0:T(8,128)}, f32[1,1176,128]{1,2,0:T(8,128)}, bf16[1,1176,128]{1,2,0:T(8,128)(2,1)S(1)}) conditional(s32[]{:T(128)} %convert_element_type.225, (bf16[1176,128]{0,1:T(8,128)(2,1)S(1)}, bf16[1176,128]{0,1:T(8,128)(2,1)S(1)}, f32[2,1176]{1,0:T(2,128)S(1)}, bf16[1176,128]{0,1:T(8,128)(2,1)S(1)}, ...), branch_computations={%region_15.16_spmd, %region_17.18_spmd} | conditional | flops 1792635520 | bytes 86619480 | solution.py:158
  441.3 18.5 %conditional.7 = (f32[1,1176,128]{1,2,0:T(8,128)}, f32[1,1176,128]{1,2,0:T(8,128)}, bf16[1,1176,128]{1,2,0:T(8,128)(2,1)S(1)}) conditional(s32[]{:T(128)} %convert_element_type.225, (bf16[1176,128]{0,1:T(8,128)(2,1)S(1)}, bf16[1176,128]{0,1:T(8,128)(2,1)S(1)}, f32[2,1176]{1,0:T(2,128)S(1)}, bf16[1176,128]{0,1:T(8,128)(2,1)S(1)}, ...), branch_computations={%region_15.16_spmd, %region_17.18_spmd} | conditional | flops 1792635520 | bytes 86619480 | solution.py:158
  467.5 18.5 %conditional.7 = (f32[1,1176,128]{1,2,0:T(8,128)}, f32[1,1176,128]{1,2,0:T(8,128)}, bf16[1,1176,128]{1,2,0:T(8,128)(2,1)S(1)}) conditional(s32[]{:T(128)} %convert_element_type.225, (bf16[1176,128]{0,1:T(8,128)(2,1)S(1)}, bf16[1176,128]{0,1:T(8,128)(2,1)S(1)}, f32[2,1176]{1,0:T(2,128)S(1)}, bf16[1176,128]{0,1:T(8,128)(2,1)S(1)}, ...), branch_computations={%region_15.16_spmd, %region_17.18_spmd} | conditional | flops 1792635520 | bytes 86619480 | solution.py:158
  493.7 18.5 %conditional.7 = (f32[1,1176,128]{1,2,0:T(8,128)}, f32[1,1176,128]{1,2,0:T(8,128)}, bf16[1,1176,128]{1,2,0:T(8,128)(2,1)S(1)}) conditional(s32[]{:T(128)} %convert_element_type.225, (bf16[1176,128]{0,1:T(8,128)(2,1)S(1)}, bf16[1176,128]{0,1:T(8,128)(2,1)S(1)}, f32[2,1176]{1,0:T(2,128)S(1)}, bf16[1176,128]{0,1:T(8,128)(2,1)S(1)}, ...), branch_computations={%region_15.16_spmd, %region_17.18_spmd} | conditional | flops 1792635520 | bytes 86619480 | solution.py:158
  566.7 5.5 copy.197
  574.4 16.4 %fusion.49 = (bf16[1176,768]{1,0:T(8,128)(2,1)}, bf16[1176,768]{1,0:T(8,128)(2,1)}) fusion(f32[1176,768]{1,0:T(8,128)} %copy.196, f32[1176,768]{1,0:T(8,128)} %copy.195, f32[1176,768]{1,0:T(8,128)} %copy.185, f32[1176,768]{1,0:T(8,128)} %copy.193, f32[768]{0:T(1024)S(1)} %copy-done.38, f32[1176,768]{1,0:T(8,128)} %copy.184, f32[1176,5376]{1,0:T(8,128)} %fusion.61, ...), kind=kLoop, calls=%fused_computation.114 | loop fusion | flops 14450688 | bytes 46970880 | tf_op jit(solution)/shard_map/convert
  590.9 20.9 %fusion.67 = (f32[3072]{0:T(1024)S(1)}, bf16[1176,3072]{1,0:T(8,128)(2,1)}) fusion(f32[1176,3072]{1,0:T(8,128)} %get-tuple-element.233, bf16[1176,768]{1,0:T(8,128)(2,1)} %param.29, bf16[3072,768]{1,0:T(8,128)(2,1)} %all-gather.8.cloned.1.call-done, f32[3072]{0:T(1024)S(1)} %copy-done.36, f32[1176,5376]{1,0:T(8,128)} %fusion.61), kind=kOutput, calls=%fused_computation.152 | convolution fusion | flops 5606863872 | bytes 42676224 | tf_op jit(solution)/shard_map/dot_general | solution.py:235
  611.8 21.5 %fusion.53 = f32[768,5376]{1,0:T(8,128)} fusion(bf16[1176,3072]{1,0:T(8,128)(2,1)} %get-tuple-element.255, bf16[1176,768]{1,0:T(8,128)(2,1)} %copy.201, bf16[1176,768]{1,0:T(8,128)(2,1)} %get-tuple-element.249, bf16[1176,768]{1,0:T(8,128)(2,1)} %get-tuple-element.248, bf16[1176,768]{1,0:T(8,128)(2,1)S(1)} %copy-done.14, f32[768]{0:T(1024)S(1)} %copy-done.42, ...), kind=kOutput, calls=%fused_computation.122 | convolution fusion | flops 9765955584 | bytes 30978240 | tf_op jit(solution)/shard_map/dot_general | solution.py:252
  635.3 18.4 %fusion.47 = (f32[1176]{0:T(1024)S(1)}, f32[1176,768]{1,0:T(8,128)}) fusion(bf16[1176,768]{1,0:T(8,128)(2,1)S(1)} %copy-done.14, f32[768]{0:T(1024)S(1)} %copy-done.42, f32[1176]{0:T(1024)S(1)} %copy-done.30, bf16[768,5376]{1,0:T(8,128)(2,1)} %all-gather.4.cloned.1.call-done, bf16[1176,3072]{1,0:T(8,128)(2,1)} %get-tuple-element.255, ...), kind=kOutput, calls=%fused_computation.112 | convolution fusion | flops 9765954560 | bytes 26333376 | tf_op jit(solution)/shard_map/dot_general | solution.py:253
  653.7 5.6 convert_add_fusion
  659.3 5.5 fusion.39
  664.9 10.9 %fusion.52 = bf16[1176,768]{1,0:T(8,128)(2,1)} fusion(f32[1176,768]{1,0:T(8,128)} %convert_add_fusion, bf16[1176,3072]{1,0:T(8,128)(2,1)} %copy-done.16, bf16[3072,768]{1,0:T(8,128)(2,1)} %all-gather.8.cloned.1.call-done, f32[768]{0:T(1024)S(1)} %convert_element_type.140), kind=kOutput, calls=%fused_computation.120 | convolution fusion | flops 5551773696 | bytes 17366016 | tf_op jit(solution)/shard_map/dot_general | solution.py:219
  679.2 161.7 %reduce-scatter.4.cloned.1.call-done = f32[48,5376]{1,0:T(8,128)} async-done(((f32[768,5376]{1,0:T(8,128)}), f32[48,5376]{1,0:T(8,128)}) %reduce-scatter.4.cloned.1.call-update) | async-done | bytes 1032208 | tf_op jit(solution)/shard_map/reduce_scatter | solution.py:267
  851.5 59.3 %all-reduce.10 = (bf16[768]{0:T(1024)(128)(2,1)S(1)}, bf16[64]{0:T(256)(128)(2,1)S(1)}, bf16[64]{0:T(256)(128)(2,1)S(1)}, bf16[3072]{0:T(1024)(128)(2,1)S(1)}, bf16[768]{0:T(1024)(128)(2,1)S(1)}) all-reduce(f32[768]{0:T(1024)S(1)} %get-tuple-element.178, f32[64]{0:T(128)S(1)} %reduce_sum.237, ...), channel_id=5, replica_groups=mesh['rep'=2,'fsdp'=16] {'fsdp'}, use_global_device_ids=true, to_apply=%region_33.34.clone | all-reduce | flops 4736 | bytes 28416
  (482 shorter events, 400.4 us)
Async XLA Ops:
  7.2 75.6 %copy-start.13 = (bf16[1176,768]{1,0:T(8,128)(2,1)S(1)}, bf16[1176,768]{1,0:T(8,128)(2,1)}, u32[]{:S(2)}) copy-start(bf16[1176,768]{1,0:T(8,128)(2,1)} %param.19) | copy-start | bytes 5419012
  7.2 84.2 %all-gather.6.cloned.1.call-start = ((), (), s32[]{:S(2)}) async-start(), calls=%async_computation.4 | async-start | bytes 1253376 | tf_op jit(solution)/shard_map/all_gather | solution.py:187
  7.9 118.4 %all-gather.4.cloned.1.call-start = ((), (), s32[]{:S(2)}) async-start(), calls=%async_computation.3 | async-start | bytes 8773632 | tf_op jit(solution)/shard_map/all_gather | solution.py:186
  8.7 582.1 %all-gather.8.cloned.1.call-start = ((), (), s32[]{:S(2)}) async-start(), calls=%async_computation.5 | async-start | bytes 5013504 | tf_op jit(solution)/shard_map/all_gather | solution.py:188
  9.4 666.4 %reduce-scatter.6.cloned.1.call-start = ((), (), s32[]{:S(2)}) async-start(), calls=%async_computation.7 | async-start | bytes 2506752 | tf_op jit(solution)/shard_map/reduce_scatter | solution.py:268
  82.8 43.5 %copy-start.41 = (f32[768]{0:T(1024)}, f32[768]{0:T(1024)S(1)}, u32[]{:S(2)}) copy-start(f32[768]{0:T(1024)S(1)} %convert_element_type.129) | copy-start | bytes 9220
  83.1 43.2 %copy-start.29 = (f32[1176]{0:T(1024)}, f32[1176]{0:T(1024)S(1)}, u32[]{:S(2)}) copy-start(f32[1176]{0:T(1024)S(1)} %broadcast_multiply_fusion.2) | copy-start | bytes 14116
  84.4 41.9 %copy-start.31 = (f32[1176]{0:T(1024)}, f32[1176]{0:T(1024)S(1)}, u32[]{:S(2)}) copy-start(f32[1176]{0:T(1024)S(1)} %fusion.57) | copy-start | bytes 14116
  85.1 121.7 %copy-start.37 = (f32[768]{0:T(1024)}, f32[768]{0:T(1024)S(1)}, u32[]{:S(2)}) copy-start(f32[768]{0:T(1024)S(1)} %mul.315) | copy-start | bytes 9220
  85.7 121.1 %copy-start.39 = (f32[768]{0:T(1024)}, f32[768]{0:T(1024)S(1)}, u32[]{:S(2)}) copy-start(f32[768]{0:T(1024)S(1)} %mul.323) | copy-start | bytes 9220
  90.0 212.9 %copy-start.35 = (f32[3072]{0:T(1024)}, f32[3072]{0:T(1024)S(1)}, u32[]{:S(2)}) copy-start(f32[3072]{0:T(1024)S(1)} %convert_element_type.138) | copy-start | bytes 36868
  158.2 33.3 %copy-start.17 = (f32[1176,12]{0,1:T(8,128)}, f32[1176,12]{0,1:T(8,128)S(1)}, u32[]{:S(2)}) copy-start(f32[1176,12]{0,1:T(8,128)S(1)} %broadcast_multiply_fusion.1) | copy-start | bytes 169348
  180.6 18.5 %copy-start.19 = (f32[1176,12]{0,1:T(8,128)}, f32[1176,12]{0,1:T(8,128)S(1)}, u32[]{:S(2)}) copy-start(f32[1176,12]{0,1:T(8,128)S(1)} %broadcast_multiply_fusion) | copy-start | bytes 169348
  302.9 37.3 %copy-start.21 = (bf16[1176,768]{1,0:T(8,128)(2,1)S(1)}, bf16[1176,768]{1,0:T(8,128)(2,1)}, u32[]{:S(2)}) copy-start(bf16[1176,768]{1,0:T(8,128)(2,1)} %param.29) | copy-start | bytes 5419012
  302.9 374.5 %reduce-scatter.8.cloned.1.call-start = ((), (), s32[]{:S(2)}) async-start(), calls=%async_computation.8 | async-start | bytes 10027008 | tf_op jit(solution)/shard_map/reduce_scatter | solution.py:269
  349.3 491.7 %reduce-scatter.4.cloned.1.call-start = ((), (), s32[]{:S(2)}) async-start(), calls=%async_computation.6 | async-start | bytes 17547264 | tf_op jit(solution)/shard_map/reduce_scatter | solution.py:267
  349.4 168.0 %copy-start.44 = (f32[64]{0:T(128)S(1)}, f32[64]{0:T(128)}, u32[]{:S(2)}) copy-start(f32[64]{0:T(128)} %convert_element_type.133) | copy-start | bytes 772
  517.4 5.6 copy-start.10
  539.4 5.6 copy-start.8
  539.4 5.6 copy-start.23
  566.7 7.7 copy-start.38
  566.7 7.7 copy-start.40
  574.4 16.4 %copy-start.36 = (f32[3072]{0:T(1024)S(1)}, f32[3072]{0:T(1024)}, u32[]{:S(2)}) copy-start(f32[3072]{0:T(1024)} %copy-done.35) | copy-start | bytes 36868
  590.8 21.0 %copy-start.14 = (bf16[1176,768]{1,0:T(8,128)(2,1)S(1)}, bf16[1176,768]{1,0:T(8,128)(2,1)}, u32[]{:S(2)}) copy-start(bf16[1176,768]{1,0:T(8,128)(2,1)} %param.19) | copy-start | bytes 5419012
  590.8 20.9 %copy-start.30 = (f32[1176]{0:T(1024)S(1)}, f32[1176]{0:T(1024)}, u32[]{:S(2)}) copy-start(f32[1176]{0:T(1024)} %copy-done.29) | copy-start | bytes 14116
  590.8 20.9 %copy-start.32 = (f32[1176]{0:T(1024)S(1)}, f32[1176]{0:T(1024)}, u32[]{:S(2)}) copy-start(f32[1176]{0:T(1024)} %copy-done.31) | copy-start | bytes 14116
  590.8 20.9 %copy-start.42 = (f32[768]{0:T(1024)S(1)}, f32[768]{0:T(1024)}, u32[]{:S(2)}) copy-start(f32[768]{0:T(1024)} %copy-done.41) | copy-start | bytes 9220
  633.3 285.4 %all-reduce.16.cloned.1.call-start = ((), (), s32[]{:S(2)}) async-start(), calls=%async_computation.9 | async-start | bytes 1769472 | tf_op jit(solution)/shard_map/psum | solution.py:286
  635.2 18.5 %copy-start.34 = (f32[1176]{0:T(1024)S(1)}, f32[1176]{0:T(1024)}, u32[]{:S(2)}) copy-start(f32[1176]{0:T(1024)} %copy-done.33) | copy-start | bytes 14116
  635.2 24.1 %copy-start.9 = (f32[6,1176,128]{1,2,0:T(8,128)S(1)}, f32[6,1176,128]{1,2,0:T(8,128)}, u32[]{:S(2)}) copy-start(f32[6,1176,128]{1,2,0:T(8,128)} %get-tuple-element.162) | copy-start | bytes 10838020
  635.2 24.1 %copy-start.11 = (f32[6,1176,128]{1,2,0:T(8,128)S(1)}, f32[6,1176,128]{1,2,0:T(8,128)}, u32[]{:S(2)}) copy-start(f32[6,1176,128]{1,2,0:T(8,128)} %get-tuple-element.163) | copy-start | bytes 10838020
  635.3 24.1 %copy-start.12 = (f32[1176,12,64]{0,2,1:T(8,128)S(1)}, f32[1176,12,64]{0,2,1:T(8,128)}, u32[]{:S(2)}) copy-start(f32[1176,12,64]{0,2,1:T(8,128)} %mul.311) | copy-start | bytes 10838020
  (41 other events, 133.7 us)
Sparse Core Ops, SparseCore 0:
  10.3 41.1 all-gather.5
  53.7 72.5 all-gather.3
  128.6 51.7 all-gather.7
  303.0 62.1 reduce-scatter.5
  369.2 110.2 reduce-scatter.7
  633.4 207.5 reduce-scatter.3
  844.0 35.6 all-reduce.15
where the time goes:
time: 941 us; the launch traced here: 931 us
  local copies, waits for them, and re-layouts  280 us (30%)
  waiting for transfers between devices  190 us (20%)
  matrix products  181 us (19%)
  blocking collectives  129 us (14%)
  other arithmetic  120 us (13%)
  between operations  20 us (2%)
  loops' own time  11.4 us (1%)
    reduce_scatter x1, waiting for transfers between devices, per_device(): lax.psum_scatter(grad_joined, 'fsdp', scatter_dimension=0, tiled=True)  162 us
    unnamed x2, blocking collectives  124 us
    reshape x42, local copies, waits for them, and re-layouts, short_path(): operand_part.reshape(images, SHORT, 2, head_size)  44.5 us
    dynamic_update_slice x30, local copies, waits for them, and re-layouts, per_device(): lax.map(partial(pair_forward, single_image), (query_pairs, key_pairs, val...  41 us
    convert_element_type x1, other arithmetic, per_device(): activated = activ_full.astype(jnp.bfloat16)  34.3 us
    dot_general x12, matrix products, short_path(): jnp.einsum('bqhd,bkhd->bhqk', query_all, key_all, preferred_element_type=...  28.9 us
    squeeze x24, local copies, waits for them, and re-layouts, per_device(): lax.map(partial(pair_forward, single_image), (query_pairs, key_pairs, val...  26.3 us
    all_gather x1, waiting for transfers between devices, per_device(): lax.all_gather(joined_weight, 'fsdp', axis=0, tiled=True)  26.3 us
  transfers between devices with their start and end apart: 7, of which 2 were waited for; matrix products, arithmetic and copies ran while one was open for 60% of the time, Pallas kernels for 0%

commit v1 on v0

v1 whole, which is shorter than its diff:
```python
import functools

import jax
import jax.numpy as jnp
from jax import lax
from jax.experimental import pallas as pl
from jax.experimental.pallas import tpu as pltpu
from jax.sharding import PartitionSpec as P

F32 = jnp.float32
BF = jnp.bfloat16
EPS = 1e-06
GROUPS = 16
SMALL = 16
HEAD = 64
PAIR = 128
CHUNK = 256
FAR = -512.0
VMEM_LIMIT = 62 << 20


def dg(left, right, left_dim, right_dim):
    return lax.dot_general(
        left, right, (((left_dim,), (right_dim,)), ((), ())), preferred_element_type=F32
    )


def spans(total, step):
    return [(start, min(step, total - start)) for start in range(0, total, step)]


def split_low(values):
    high = values.astype(BF)
    return high, (values - high.astype(F32)).astype(BF)


def block_ones(size, scale, flip=0):
    row = lax.broadcasted_iota(jnp.int32, (size, size), 0) // HEAD
    col = lax.broadcasted_iota(jnp.int32, (size, size), 1) // HEAD
    return jnp.where(row == (col ^ flip), scale, 0.0).astype(BF)


def head_sum(values, ones):
    high, low = split_low(values)
    return dg(high, ones, 1, 0) + dg(low, ones, 1, 0)


def row_norm(rows):
    mean = jnp.mean(rows, axis=-1, keepdims=True)
    centered = rows - mean
    variance = jnp.mean(centered * centered, axis=-1, keepdims=True)
    inverse = lax.rsqrt(variance + EPS)
    return centered * inverse, inverse


def small_rows(small_ref):
    return jnp.sum(small_ref[...].astype(F32), axis=0)


def square(block_ref):
    groups, rows, width = block_ref.shape
    return block_ref[...].reshape(groups * rows, width)


def params(steps):
    return pltpu.CompilerParams(
        dimension_semantics=("arbitrary",) * steps, vmem_limit_bytes=VMEM_LIMIT
    )


def cost(flops, moved, special=0):
    return pl.CostEstimate(flops=int(flops), bytes_accessed=int(moved), transcendentals=int(special))


def project_kernel(token_ref, weight_ref, small_ref, low_ref, hat_ref, inv_ref, normed_ref, pre_ref):
    section = pl.program_id(0)
    rows = small_rows(small_ref)

    @pl.when(section == 0)
    def _():
        for start, size in spans(token_ref.shape[0], CHUNK):
            hat, _ = row_norm(token_ref[start : start + size, :].astype(F32))
            normed_ref[start : start + size, :] = (hat * rows[0:1, :]).astype(BF)

    weight = square(weight_ref)

    @pl.when(section < 2)
    def _():
        ones = block_ones(2 * PAIR, 1.0 / HEAD)
        gain_pair = jnp.where(section == 0, rows[6:7, :PAIR], rows[6:7, PAIR : 2 * PAIR])
        gain = jnp.concatenate([gain_pair, gain_pair], axis=1)
        factor = jnp.where(section == 0, HEAD**-0.5, 1.0).astype(F32)
        for start, size in spans(token_ref.shape[0], CHUNK):
            part = slice(start, start + size)
            pre_ref[:size, :] = dg(normed_ref[part, :], weight, 1, 0)
            for left, wide in spans(pre_ref.shape[1], 2 * PAIR):
                lanes = slice(left, left + wide)
                pre = pre_ref[:size, lanes]
                centered = pre - head_sum(pre, ones)
                inverse = lax.rsqrt(head_sum(centered * centered, ones) + EPS)
                hat = centered * inverse
                hat_ref[0, part, lanes] = hat
                inv_ref[0, part, lanes] = inverse
                low_ref[0, part, lanes] = ((hat * gain).astype(BF).astype(F32) * factor).astype(BF)

    @pl.when(section == 2)
    def _():
        for start, size in spans(token_ref.shape[0], CHUNK):
            part = slice(start, start + size)
            low_ref[0, part, :] = dg(normed_ref[part, :], weight, 1, 0).astype(BF)


def project(tokens, gathered):
    length, width = tokens.shape
    rows = width // GROUPS
    full = pl.BlockSpec((length, width), lambda s: (0, 0))
    return pl.pallas_call(
        project_kernel,
        grid=(3,),
        in_specs=[
            full,
            pl.BlockSpec((GROUPS, rows, width), lambda s: (0, s, 0)),
            pl.BlockSpec((GROUPS, SMALL, width), lambda s: (0, 4 * rows // SMALL, 0)),
        ],
        out_specs=[
            pl.BlockSpec((1, length, width), lambda s: (s, 0, 0)),
            pl.BlockSpec((1, length, width), lambda s: (jnp.minimum(s, 1), 0, 0)),
            pl.BlockSpec((1, length, width), lambda s: (jnp.minimum(s, 1), 0, 0)),
            full,
        ],
        out_shape=[
            jax.ShapeDtypeStruct((3, length, width), BF),
            jax.ShapeDtypeStruct((2, length, width), F32),
            jax.ShapeDtypeStruct((2, length, width), F32),
            jax.ShapeDtypeStruct((length, width), BF),
        ],
        scratch_shapes=[pltpu.VMEM((CHUNK, width), F32)],
        compiler_params=params(1),
        cost_estimate=cost(9 * length * width * width, 40 * length * width),
        name="project",
    )(tokens, gathered, gathered)


def own_lanes(length, head):
    lane = lax.broadcasted_iota(jnp.int32, (length, PAIR), 1)
    return (lane // HEAD) == head


def attend_kernel(query_ref, key_ref, value_ref, near_ref, far_ref, exps_ref, mixed_ref, wide_ref, inv_ref):
    length = query_ref.shape[1]
    values = jnp.concatenate([value_ref[0], jnp.ones((length, PAIR), BF)], axis=1)
    for head in range(2):
        own = own_lanes(length, head)
        keys = jnp.where(own, key_ref[0], far_ref[...])
        for start, size in spans(length, CHUNK):
            part = slice(start, start + size)
            own_part = own_lanes(size, head)
            queries = jnp.where(own_part, query_ref[0, part, :], near_ref[part, :])
            exps = jnp.exp(dg(queries, keys, 1, 1)).astype(BF)
            exps_ref[head, part, :] = exps
            both = dg(exps, values, 1, 0)
            inverse = 1.0 / both[:, PAIR:]
            out = both[:, :PAIR] * inverse
            if head == 1:
                out = jnp.where(own_part, out, wide_ref[part, :])
                inverse = jnp.where(own_part, inverse, inv_ref[part, :])
                mixed_ref[part, :] = out.astype(BF)
            wide_ref[part, :] = out
            inv_ref[part, :] = inverse


def attend(low, near, far):
    _, length, width = low.shape
    pairs = width // PAIR
    lanes = pl.BlockSpec((length, PAIR), lambda p: (0, p))
    fixed = pl.BlockSpec((length, PAIR), lambda p: (0, 0))
    return pl.pallas_call(
        attend_kernel,
        grid=(pairs,),
        in_specs=[pl.BlockSpec((1, length, PAIR), lambda p, k=k: (k, 0, p)) for k in range(3)]
        + [fixed, fixed],
        out_specs=[pl.BlockSpec((2, length, length), lambda p: (p, 0, 0)), lanes, lanes, lanes],
        out_shape=[
            jax.ShapeDtypeStruct((2 * pairs, length, length), BF),
            jax.ShapeDtypeStruct((length, width), BF),
            jax.ShapeDtypeStruct((length, width), F32),
            jax.ShapeDtypeStruct((length, width), F32),
        ],
        compiler_params=params(1),
        cost_estimate=cost(pairs * 2 * 8 * PAIR * length * length, 24 * length * length),
        name="attend",
    )(low, low, low, near, far)


def mlp_kernel(
    normed_ref,
    cot_ref,
    up_ref,
    down_ref,
    small_ref,
    branch_ref,
    back_ref,
    hidden_ref,
    grads_ref,
    small_s,
    act_s,
    grad_s,
    up_s,
    down_s,
    sems,
):
    step = pl.program_id(0)
    length, width = normed_ref.shape
    rows = width // GROUPS
    small_s[...] = small_rows(small_ref)
    bias = small_s[pl.ds(2 + step, 1), :]
    up = square(up_ref)
    down = square(down_ref)
    hidden = jnp.zeros((1, width), F32)
    for start, size in spans(length, CHUNK):
        part = slice(start, start + size)
        inner = dg(normed_ref[part, :], up, 1, 0) + bias
        cdf = 0.5 + 0.5 * lax.erf(inner * (0.5**0.5))
        pdf = jnp.exp(inner * inner * -0.5) * 0.3989422804014327
        act = (inner * cdf).astype(BF)
        grad = dg(cot_ref[part, :], down, 1, 1) * (cdf + inner * pdf)
        hidden = hidden + jnp.sum(grad, axis=0, keepdims=True)
        grad_low = grad.astype(BF)
        act_s[part, :] = act
        grad_s[part, :] = grad_low
        forward = dg(act, down, 1, 0)
        backward = dg(grad_low, up, 1, 1)

        @pl.when(step == 0)
        def _():
            branch_ref[part, :] = forward
            back_ref[part, :] = backward

        @pl.when(step > 0)
        def _():
            branch_ref[part, :] = branch_ref[part, :] + forward
            back_ref[part, :] = back_ref[part, :] + backward

    hidden_ref[0] = hidden
    groups = GROUPS // pl.num_programs(0)

    def copies(index):
        return (
            pltpu.make_async_copy(
                up_s, grads_ref.at[:, pl.ds(pl.multiple_of(index * rows, rows), rows), :], sems.at[0]
            ),
            pltpu.make_async_copy(
                down_s,
                grads_ref.at[pl.ds(index * groups, groups), pl.ds(4 * rows, 4 * rows), :],
                sems.at[1],
            ),
        )

    @pl.when(step > 0)
    def _():
        for copy in copies(step - 1):
            copy.wait()

    up_s[...] = dg(normed_ref[...], grad_s[...], 0, 0).astype(BF).reshape(up_s.shape)
    down_s[...] = dg(act_s[...], cot_ref[...], 0, 0).astype(BF).reshape(down_s.shape)
    for copy in copies(step):
        copy.start()

    @pl.when(step == pl.num_programs(0) - 1)
    def _():
        for copy in copies(step):
            copy.wait()


def mlp(normed, cotangent, gathered, gathered_small):
    length, width = normed.shape
    rows = width // GROUPS
    steps = 4
    full = pl.BlockSpec((length, width), lambda s: (0, 0))
    return pl.pallas_call(
        mlp_kernel,
        grid=(steps,),
        in_specs=[
            full,
            full,
            pl.BlockSpec((GROUPS, rows, width), lambda s: (0, s, 0)),
            pl.BlockSpec((GROUPS // steps, steps * rows, width), lambda s: (s, 1, 0)),
            pl.BlockSpec((GROUPS, SMALL, width), lambda s: (0, 4 * rows // SMALL, 0)),
        ],
        out_specs=[
            full,
            full,
            pl.BlockSpec((1, 1, width), lambda s: (s, 0, 0)),
            pl.BlockSpec(memory_space=pl.ANY),
        ],
        out_shape=[
            jax.ShapeDtypeStruct((length, width), F32),
            jax.ShapeDtypeStruct((length, width), F32),
            jax.ShapeDtypeStruct((steps, 1, width), F32),
            jax.ShapeDtypeStruct((GROUPS, 8 * rows, width), BF),
        ],
        scratch_shapes=[
            pltpu.VMEM((SMALL, width), F32),
            pltpu.VMEM((length, width), BF),
            pltpu.VMEM((length, width), BF),
            pltpu.VMEM((GROUPS, rows, width), BF),
            pltpu.VMEM((GROUPS // steps, steps * rows, width), BF),
            pltpu.SemaphoreType.DMA((2,)),
        ],
        compiler_params=params(1),
        cost_estimate=cost(48 * length * width * width, 40 * length * width, 8 * length * width),
        name="mlp",
    )(normed, cotangent, gathered, gathered, gathered_small)


def backward_kernel(
    query_ref,
    key_ref,
    value_ref,
    exps_ref,
    wide_ref,
    inv_ref,
    cot_ref,
    heads_ref,
    small_ref,
    qhat_ref,
    khat_ref,
    qinv_ref,
    kinv_ref,
    grad_ref,
    sums_ref,
    heads_s,
    dot_s,
    delta_s,
    query_s,
    key_s,
    value_s,
):
    pair = pl.program_id(0)
    length = query_ref.shape[1]

    @pl.when(pair == 0)
    def _():
        heads_s[...] = square(heads_ref)
        sums_ref[...] = jnp.zeros_like(sums_ref)

    rows = small_rows(small_ref)
    flipped = block_ones(PAIR, 1.0, 1)
    head_rows = heads_s[pl.ds(pl.multiple_of(pair * PAIR, PAIR), PAIR), :]
    for start, size in spans(length, CHUNK):
        part = slice(start, start + size)
        grad = dg(cot_ref[part, :], head_rows, 1, 1) * inv_ref[part, :]
        low = grad.astype(BF)
        dot_s[part, :] = low
        delta_s[part, :] = head_sum(low.astype(F32) * wide_ref[part, :], flipped)

    for head in range(2):
        lane = lax.broadcasted_iota(jnp.int32, (length, PAIR), 1)
        own = (lane // HEAD) == head
        values = jnp.where(own, value_ref[0], jnp.where(lane % HEAD < 2, 1.0, 0.0).astype(BF))
        for start, size in spans(length, CHUNK):
            part = slice(start, start + size)
            lane_p = lax.broadcasted_iota(jnp.int32, (size, PAIR), 1)
            own_p = (lane_p // HEAD) == head
            high, rest = split_low(-delta_s[part, :])
            extra = jnp.where(
                lane_p % HEAD == 0, high, jnp.where(lane_p % HEAD == 1, rest, jnp.zeros_like(rest))
            )
            dots = dot_s[part, :]
            slopes = dg(jnp.where(own_p, dots, extra), values, 1, 1)
            exps = exps_ref[head, part, :]
            scores = (exps.astype(F32) * slopes).astype(BF)
            dq = dg(scores, key_ref[0], 1, 0)
            dk = dg(scores, query_ref[0, part, :], 0, 0)
            dv = dg(exps, dots, 0, 0)
            if head == 1:
                dq = jnp.where(own_p, dq, query_s[part, :])
            query_s[part, :] = dq
            if start == 0:
                key_s[head] = dk
                value_s[head] = dv
            else:
                key_s[head] = key_s[head] + dk
                value_s[head] = value_s[head] + dv

    ones = block_ones(PAIR, 1.0 / HEAD)
    for start, size in spans(length, CHUNK):
        part = slice(start, start + size)
        own_p = own_lanes(size, 0)
        both = (
            (query_s[part, :] * HEAD**-0.5, qhat_ref, qinv_ref, rows[6:7, :PAIR]),
            (
                jnp.where(own_p, key_s[0, part, :], key_s[1, part, :]),
                khat_ref,
                kinv_ref,
                rows[6:7, PAIR : 2 * PAIR],
            ),
        )
        for index, (grad, hat_ref, inverse_ref, gain) in enumerate(both):
            hat = hat_ref[0, part, :]
            product = grad * hat
            sums_ref[index : index + 1, :] += jnp.sum(product, axis=0, keepdims=True)
            mean = head_sum(grad * gain, ones)
            along = head_sum(product * gain, ones)
            grad_ref[index, part, :] = (
                inverse_ref[0, part, :] * (grad * gain - mean - hat * along)
            ).astype(BF)
        grad_ref[2, part, :] = jnp.where(own_p, value_s[0, part, :], value_s[1, part, :]).astype(BF)


def attend_back(low, exps, wide, inverse, cotangent, gathered, hat, inv):
    _, length, width = low.shape
    rows = width // GROUPS
    pairs = width // PAIR
    lanes = pl.BlockSpec((length, PAIR), lambda p: (0, p))

    def third(k):
        return pl.BlockSpec((1, length, PAIR), lambda p: (k, 0, p))

    return pl.pallas_call(
        backward_kernel,
        grid=(pairs,),
        in_specs=[third(k) for k in range(3)]
        + [
            pl.BlockSpec((2, length, length), lambda p: (p, 0, 0)),
            lanes,
            lanes,
            pl.BlockSpec((length, width), lambda p: (0, 0)),
            pl.BlockSpec((GROUPS, rows, width), lambda p: (0, 3, 0)),
            pl.BlockSpec((GROUPS, SMALL, width), lambda p: (0, 4 * rows // SMALL, 0)),
            third(0),
            third(1),
            third(0),
            third(1),
        ],
        out_specs=[
            pl.BlockSpec((3, length, PAIR), lambda p: (0, 0, p)),
            pl.BlockSpec((8, PAIR), lambda p: (0, 0)),
        ],
        out_shape=[
            jax.ShapeDtypeStruct((3, length, width), BF),
            jax.ShapeDtypeStruct((8, PAIR), F32),
        ],
        scratch_shapes=[
            pltpu.VMEM((width, width), BF),
            pltpu.VMEM((length, PAIR), BF),
            pltpu.VMEM((length, PAIR), F32),
            pltpu.VMEM((length, PAIR), F32),
            pltpu.VMEM((2, length, PAIR), F32),
            pltpu.VMEM((2, length, PAIR), F32),
        ],
        compiler_params=params(1),
        cost_estimate=cost(pairs * 2 * 16 * PAIR * length * length, 24 * length * length),
        name="attend_back",
    )(low, low, low, exps, wide, inverse, cotangent, gathered, gathered, hat, hat, inv, inv)


def weights_kernel(normed_ref, grad_ref, mixed_ref, cot_ref, out_ref):
    section = pl.program_id(0)

    @pl.when(section < 3)
    def _():
        out_ref[...] = dg(normed_ref[...], grad_ref[0], 0, 0).astype(BF).reshape(out_ref.shape)

    @pl.when(section == 3)
    def _():
        out_ref[...] = dg(mixed_ref[...], cot_ref[...], 0, 0).astype(BF).reshape(out_ref.shape)


def weight_grads(normed, grads, mixed, cotangent):
    _, length, width = grads.shape
    rows = width // GROUPS
    full = pl.BlockSpec((length, width), lambda s: (0, 0))
    return pl.pallas_call(
        weights_kernel,
        grid=(4,),
        in_specs=[
            full,
            pl.BlockSpec((1, length, width), lambda s: (jnp.minimum(s, 2), 0, 0)),
            full,
            full,
        ],
        out_specs=pl.BlockSpec((GROUPS, rows, width), lambda s: (0, s, 0)),
        out_shape=jax.ShapeDtypeStruct((GROUPS, 4 * rows, width), BF),
        compiler_params=params(1),
        cost_estimate=cost(8 * length * width * width, 14 * length * width),
        name="weight_grads",
    )(normed, grads, mixed, cotangent)


def tail_kernel(
    grad_ref,
    weight_ref,
    small_ref,
    token_ref,
    cot_ref,
    mixed_ref,
    branch_ref,
    back_ref,
    out_ref,
    token_grad_ref,
    total_s,
):
    section = pl.program_id(0)
    length = token_ref.shape[0]
    weight = square(weight_ref)

    @pl.when(section == 0)
    def _():
        for start, size in spans(length, CHUNK):
            part = slice(start, start + size)
            total_s[part, :] = back_ref[part, :] + dg(grad_ref[0, part, :], weight, 1, 1)

    @pl.when((section > 0) & (section < 3))
    def _():
        for start, size in spans(length, CHUNK):
            part = slice(start, start + size)
            total_s[part, :] = total_s[part, :] + dg(grad_ref[0, part, :], weight, 1, 1)

    @pl.when(section == 3)
    def _():
        rows = small_rows(small_ref)
        for start, size in spans(length, CHUNK):
            part = slice(start, start + size)
            tokens = token_ref[part, :].astype(F32)
            attended = dg(mixed_ref[part, :], weight, 1, 0)
            out_ref[part, :] = (tokens + attended + branch_ref[part, :] + rows[1:2, :]).astype(BF)
            hat, inverse = row_norm(tokens)
            grad = total_s[part, :] * rows[0:1, :]
            mean = jnp.mean(grad, axis=-1, keepdims=True)
            along = jnp.mean(grad * hat, axis=-1, keepdims=True)
            token_grad_ref[part, :] = (
                cot_ref[part, :].astype(F32) + inverse * (grad - mean - hat * along)
            ).astype(BF)


def tail(grads, gathered, tokens, cotangent, mixed, branch, back):
    _, length, width = grads.shape
    rows = width // GROUPS
    full = pl.BlockSpec((length, width), lambda s: (0, 0))
    return pl.pallas_call(
        tail_kernel,
        grid=(4,),
        in_specs=[
            pl.BlockSpec((1, length, width), lambda s: (jnp.minimum(s, 2), 0, 0)),
            pl.BlockSpec((GROUPS, rows, width), lambda s: (0, s, 0)),
            pl.BlockSpec((GROUPS, SMALL, width), lambda s: (0, 4 * rows // SMALL, 0)),
            full,
            full,
            full,
            full,
            full,
        ],
        out_specs=[full, full],
        out_shape=[
            jax.ShapeDtypeStruct((length, width), BF),
            jax.ShapeDtypeStruct((length, width), BF),
        ],
        scratch_shapes=[pltpu.VMEM((length, width), F32)],
        compiler_params=params(1),
        cost_estimate=cost(8 * length * width * width, 24 * length * width),
        name="tail",
    )(grads, gathered, gathered, tokens, cotangent, mixed, branch, back)


def place(vector, offset, total):
    return lax.dynamic_update_slice(jnp.zeros((total,), vector.dtype), vector, (offset,))


def stack_columns(shard, first, count, width):
    return [shard[:, (first + k) * width : (first + k + 1) * width] for k in range(count)]


def regroup(gathered, section_rows):
    devices, _, width = gathered.shape
    if devices == GROUPS:
        return gathered
    fold = devices // GROUPS
    parts, start = [], 0
    for rows, small in section_rows:
        piece = gathered[:, start : start + rows, :]
        start += rows
        if small:
            parts.append(piece.reshape(GROUPS, fold, rows, width).sum(1))
        else:
            parts.append(piece.reshape(GROUPS, fold * rows, width))
    return jnp.concatenate(parts, axis=1)


def ungroup(grouped, section_rows, devices):
    if devices == GROUPS:
        return grouped
    fold = devices // GROUPS
    width = grouped.shape[2]
    parts, start = [], 0
    for rows, small in section_rows:
        wide = rows if small else rows * fold
        piece = grouped[:, start : start + wide, :]
        start += wide
        if small:
            parts.append(jnp.repeat(piece, fold, axis=0))
        else:
            parts.append(piece.reshape(devices, rows, width))
    return jnp.concatenate(parts, axis=1)


def per_device(
    devices,
    tokens_in,
    token_image,
    joined_weight,
    heads_weight,
    down_weight,
    norm_gain,
    query_gain,
    key_gain,
    hidden_bias,
    output_bias,
    cotangent,
):
    length, width = tokens_in.shape
    rows = joined_weight.shape[0]
    me = lax.axis_index("fsdp")
    thin, bias_thin, head_thin = norm_gain.shape[0], hidden_bias.shape[0], query_gain.shape[0]

    small = (
        place(norm_gain, me * thin, SMALL * width)
        + place(output_bias, width + me * thin, SMALL * width)
        + place(hidden_bias, 2 * width + me * bias_thin, SMALL * width)
    )
    for index, vector in enumerate((query_gain, query_gain, key_gain, key_gain)):
        small = small + place(vector, 6 * width + index * HEAD + me * head_thin, SMALL * width)
    first_rows = [(rows, False)] * 4 + [(SMALL, True)]
    first = jnp.concatenate(
        stack_columns(joined_weight, 0, 3, width) + [heads_weight, small.reshape(SMALL, width)], axis=0
    )
    gathered = regroup(lax.all_gather(first, "fsdp", axis=0), first_rows)

    second_rows = [(rows, False)] * 4 + [(4 * rows, False)]
    second = jnp.concatenate(stack_columns(joined_weight, 3, 4, width) + [down_weight], axis=0)
    second, _ = lax.optimization_barrier((second, gathered[0, 0, 0]))
    gathered_mlp = regroup(lax.all_gather(second, "fsdp", axis=0), second_rows)

    lane = lax.broadcasted_iota(jnp.int32, (length, PAIR), 1) % HEAD
    same = lane == token_image[:, None]
    near = jnp.where(same, 1.0, 0.0).astype(BF)
    far = jnp.where(same | (lane >= 6), 0.0, FAR).astype(BF)

    low, hat, inv, normed = project(tokens_in, gathered)
    exps, mixed, wide, inverse = attend(low, near, far)
    branch, back, hidden, mlp_grads = mlp(normed, cotangent, gathered_mlp, gathered)

    owner = lax.broadcasted_iota(jnp.int32, (GROUPS, 1, width), 0)
    at = lax.broadcasted_iota(jnp.int32, (GROUPS, 1, width), 2)
    per_group = width // GROUPS
    grad_output = jnp.sum(cotangent.astype(F32), axis=0)[None, None, :]
    vectors = [jnp.where(at // per_group == owner, grad_output, 0.0)]
    for k in range(4):
        block = at // (4 * per_group) + k * (GROUPS // 4)
        vectors.append(jnp.where(block == owner, hidden[k][None], 0.0))
    vectors.append(jnp.zeros((GROUPS, SMALL - 5, width), F32))
    early_small = jnp.concatenate(vectors, axis=1).astype(BF)

    grads, sums = attend_back(low, exps, wide, inverse, cotangent, gathered, hat, inv)
    late_grads = weight_grads(normed, grads, mixed, cotangent)
    query_sum = sums[0, :HEAD] + sums[0, HEAD:]
    key_sum = sums[1, :HEAD] + sums[1, HEAD:]
    packed = jnp.pad(jnp.concatenate([query_sum, key_sum]), (0, width - 2 * HEAD))[None, None, :]
    late_small = jnp.where((at % HEAD) // (HEAD // GROUPS) == owner, packed, 0.0)
    late_small = jnp.pad(late_small, ((0, 0), (0, SMALL - 1), (0, 0))).astype(BF)
    block_out, grad_tokens = tail(grads, gathered, tokens_in, cotangent, mixed, branch, back)

    def reduce(array, section_rows):
        array = ungroup(array, section_rows, devices)
        return lax.psum_scatter(array, "fsdp", scatter_dimension=0, tiled=True)[0]

    def both(array):
        return lax.psum(array, "rep").astype(F32)

    mlp_total = both(reduce(mlp_grads, second_rows))
    late_total = both(reduce(late_grads, first_rows[:4]))
    small_total = both(
        reduce(jnp.concatenate([early_small, late_small], axis=1), [(2 * SMALL, True)])
    )

    total_joined = jnp.concatenate(
        [late_total[k * rows : (k + 1) * rows] for k in range(3)]
        + [mlp_total[k * rows : (k + 1) * rows] for k in range(4)],
        axis=1,
    )
    total_heads = late_total[3 * rows : 4 * rows]
    total_down = mlp_total[4 * rows :]
    total_norm = jnp.sum(joined_weight.astype(F32) * total_joined, axis=1) / norm_gain.astype(F32)

    def take(row, offset, size):
        return lax.dynamic_slice(small_total, (row, offset), (1, size))[0]

    flat = me * bias_thin
    total_output = take(0, me * thin, thin)
    total_hidden = take(1 + flat // width, flat % width, bias_thin)
    total_query = take(SMALL, me * head_thin, head_thin)
    total_key = take(SMALL, HEAD + me * head_thin, head_thin)
    return (
        block_out,
        grad_tokens,
        total_joined,
        total_heads,
        total_down,
        total_norm,
        total_query,
        total_key,
        total_hidden,
        total_output,
    )


def solution(mesh):
    tokens, shard, thin = P(("rep", "fsdp"), None), P("fsdp", None), P("fsdp")
    return jax.shard_map(
        functools.partial(per_device, mesh.shape["fsdp"]),
        mesh=mesh,
        in_specs=(tokens, P(("rep", "fsdp")), shard, shard, shard, thin, thin, thin, thin, thin, tokens),
        out_specs=(tokens, tokens, shard, shard, shard, thin, thin, thin, thin, thin),
        check_vma=False,
    )
```

time: 941 us -> 500 us (0.53)
  local copies, waits for them, and re-layouts: 280 us -> 23.1 us
  matrix products: 181 us -> 0 us
  Pallas kernels: 0 us -> 181 us
  blocking collectives: 129 us -> 9.57 us
  other arithmetic: 120 us -> 10 us
  waiting for transfers between devices: 190 us -> 251 us
  loops' own time: 11.4 us -> 0 us
    pallas_call x0 -> x6, Pallas kernels: none -> 181 us  [the longest x1 59.4 us: attend_back(): pl.pallas_call(backward_kernel, grid=(pairs,), in_specs=[third(k) for k i...]
    dot_general x51 -> x0, matrix products: 181 us -> none  [the longest x12 28.9 us: short_path(): jnp.einsum('bqhd,bkhd->bhqk', query_all, key_all, preferred_element_type=...]
    unnamed x2 -> x0, blocking collectives: 124 us -> none
    convert_element_type x24 -> x4, other arithmetic: 62 us -> 3.94 us  [the longest x3 2.2 us: both(): return lax.psum(array, 'rep').astype(F32)]
    broadcast_in_dim x38 -> x1, local copies, waits for them, and re-layouts: 53.1 us -> 0.03 us  [per_device(): vectors.append(jnp.zeros((GROUPS, SMALL - 5, width), F32))]
    reshape x49 -> x1, local copies, waits for them, and re-layouts: 47.3 us -> 0.05 us  [per_device(): small.reshape(SMALL, width)]
    dynamic_update_slice x30 -> x1, local copies, waits for them, and re-layouts: 41 us -> 0.86 us  [place(): lax.dynamic_update_slice(jnp.zeros((total,), vector.dtype), vector, (offs...]
    reduce_sum x21 -> x2, other arithmetic: 39.1 us -> 0.55 us  [the longest x1 0.33 us: per_device(): grad_output = jnp.sum(cotangent.astype(F32), axis=0)[None, None, :]]
  transfers between devices with their start and end apart: 7 -> 6, of which waited for: 2 -> 5; matrix products, arithmetic and copies ran while one was open for 60% -> 3% of each run, Pallas kernels for 0% -> 37%
where the time goes in v1:
time: 500 us; the launch traced here: 490 us
  waiting for transfers between devices  251 us (50%)
  Pallas kernels  181 us (36%)
  local copies, waits for them, and re-layouts  23.1 us (5%)
  between operations  14.9 us (3%)
  other arithmetic  10 us (2%)
  blocking collectives  9.57 us (2%)
    reduce_scatter x3, waiting for transfers between devices, reduce(): return lax.psum_scatter(array, 'fsdp', scatter_dimension=0, tiled=True)[0]  171 us
    pallas_call x1, Pallas kernels, attend_back(): pl.pallas_call(backward_kernel, grid=(pairs,), in_specs=[third(k) for k i...  59.4 us
    all_gather x1, waiting for transfers between devices, per_device(): gathered = regroup(lax.all_gather(first, 'fsdp', axis=0), first_rows)  54.2 us
    pallas_call x1, Pallas kernels, mlp(): pl.pallas_call(mlp_kernel, grid=(steps,), in_specs=[full, full, pl.BlockS...  51.4 us
    psum x1, waiting for transfers between devices, both(): return lax.psum(array, 'rep').astype(F32)  26.4 us
    pallas_call x1, Pallas kernels, attend(): pl.pallas_call(attend_kernel, grid=(pairs,), in_specs=[pl.BlockSpec((1, l...  25 us
    pallas_call x1, Pallas kernels, project(): pl.pallas_call(project_kernel, grid=(3,), in_specs=[full, pl.BlockSpec((G...  17.3 us
    pallas_call x1, Pallas kernels, tail(): pl.pallas_call(tail_kernel, grid=(4,), in_specs=[pl.BlockSpec((1, length,...  16.9 us
  transfers between devices with their start and end apart: 6, of which 5 were waited for; matrix products, arithmetic and copies ran while one was open for 3% of the time, Pallas kernels for 37%

profile of v1, /device:TPU:0, one launch (start us, length us, event | category | flops | bytes accessed | tf_op | source)
XLA Modules:
  0.0 490.5 jit_solution(8963107236801952215)
XLA Ops:
  7.2 0.9 dynamic_update_slice.23
  8.1 0.7 dynamic-slice_add_fusion.5
  9.0 0.7 dynamic-slice_add_fusion.4
  9.9 0.7 dynamic-slice_add_fusion.3
  10.9 0.7 dynamic-slice_add_fusion.2
  11.8 0.7 dynamic-slice_add_fusion.1
  12.7 0.7 dynamic-slice_add_fusion
  13.7 0.9 slice_dynamic-update-slice_fusion.10
  14.5 0.9 slice_dynamic-update-slice_fusion.9
  15.5 0.9 slice_dynamic-update-slice_fusion.8
  16.4 0.9 slice_dynamic-update-slice_fusion.7
  17.4 0.9 constant_dynamic-update-slice_fusion.1
  19.0 1.0 constant_dynamic-update-slice_fusion.2
  20.0 0.8 copy-done.3
  20.9 1.7 select_convert_fusion
  22.7 54.2 %all-gather.5.cloned.1.call-done = bf16[3328,768]{1,0:T(8,128)(2,1)} async-done(((bf16[208,768]{1,0:T(8,128)(2,1)}), bf16[3328,768]{1,0:T(8,128)(2,1)}) %all-gather.5.cloned.1.call-update) | async-done | bytes 5111824 | tf_op jit(solution)/shard_map/all_gather | solution.py:637
  76.9 17.3 %project.1 = (bf16[3,1176,768]{2,1,0:T(8,128)(2,1)}, f32[2,1176,768]{2,1,0:T(8,128)}, f32[2,1176,768]{2,1,0:T(8,128)}, bf16[1176,768]{1,0:T(8,128)(2,1)}) custom-call(bf16[1176,768]{1,0:T(8,128)(2,1)} %token_ref.3, bf16[16,208,768]{2,1,0:T(8,128)(2,1)} %bitcast.16, bf16[16,208,768]{2,1,0:T(8,128)(2,1)} %bitcast.17), custom_call_target="tpu_custom_call" | custom-call | flops 6242697216 | bytes 36126720 | tf_op jit(solution)/shard_map/project/pallas_call | solution.py:117
  94.3 25.0 %attend.1 = (bf16[12,1176,1176]{2,1,0:T(8,128)(2,1)}, bf16[1176,768]{1,0:T(8,128)(2,1)}, f32[1176,768]{1,0:T(8,128)}, f32[1176,768]{1,0:T(8,128)}) custom-call(bf16[3,1176,768]{2,1,0:T(8,128)(2,1)} %get-tuple-element.26.query_ref.key_ref.value_ref, bf16[3,1176,768]{2,1,0:T(8,128)(2,1)} %get-tuple-element.26.query_ref.key_ref.value_ref, ...), custom_call_target="tpu_custom_call" | custom-call | flops 16994009088 | bytes 33191424 | tf_op jit(solution)/shard_map/attend/pallas_call | solution.py:177
  119.3 59.4 %attend_back.1 = (bf16[3,1176,768]{2,1,0:T(8,128)(2,1)}, f32[8,128]{1,0:T(8,128)}) custom-call(bf16[3,1176,768]{2,1,0:T(8,128)(2,1)} %get-tuple-element.26.query_ref.key_ref.value_ref, bf16[3,1176,768]{2,1,0:T(8,128)(2,1)} %get-tuple-element.26.query_ref.key_ref.value_ref, bf16[3,1176,768]{2,1,0:T(8,128)(2,1)} %get-tuple-element.26.query_ref.key_ref.value_ref, ...), custom_call_target="tpu_custom_call" | custom-call | flops 33988018176 | bytes 33191424 | tf_op jit(solution)/shard_map/attend_back/pallas_call | solution.py:420
  178.7 11.4 %weight_grads.1 = bf16[16,192,768]{2,1,0:T(8,128)(2,1)} custom-call(bf16[1176,768]{1,0:T(8,128)(2,1)} %get-tuple-element.34.normed_ref, bf16[3,1176,768]{2,1,0:T(8,128)(2,1)} %get-tuple-element.32.grad_ref, bf16[1176,768]{1,0:T(8,128)(2,1)} %get-tuple-element.33.mixed_ref, bf16[1176,768]{1,0:T(8,128)(2,1)} %cot_ref.7), custom_call_target="tpu_custom_call" | custom-call | flops 5549064192 | bytes 12644352 | tf_op jit(solution)/shard_map/weight_grads/pallas_call | solution.py:474
  190.2 51.4 %mlp.1 = (f32[1176,768]{1,0:T(8,128)}, f32[1176,768]{1,0:T(8,128)}, f32[4,1,768]{2,1,0:T(1,128)}, bf16[16,384,768]{2,1,0:T(8,128)(2,1)}) custom-call(bf16[1176,768]{1,0:T(8,128)(2,1)} %get-tuple-element.34.normed_ref, bf16[1176,768]{1,0:T(8,128)(2,1)} %cot_ref.7, bf16[16,384,768]{2,1,0:T(8,128)(2,1)} %bitcast.27, bf16[16,384,768]{2,1,0:T(8,128)(2,1)} %bitcast.28, ...), custom_call_target="tpu_custom_call" | custom-call | flops 33294385152 | bytes 36126720 | tf_op jit(solution)/shard_map/mlp/pallas_call | solution.py:280
  241.8 1.3 copy-done
  244.1 8.0 %concatenate.22 = bf16[16,32,768]{2,1,0:T(8,128)(2,1)} concatenate(bf16[16,1,768]{2,1,0:T(2,128)(2,1)S(1)} %fusion.12, bf16[16,1,768]{2,1,0:T(2,128)(2,1)S(1)} %get-tuple-element.61, bf16[16,1,768]{2,1,0:T(2,128)(2,1)S(1)} %get-tuple-element.59, bf16[16,1,768]{2,1,0:T(2,128)(2,1)S(1)} %get-tuple-element.60, bf16[16,1,768]{2,1,0:T(2,128)(2,1)S(1)} %get-tuple-element.58, ...), dimensions={1} | concatenate | bytes 1572864 | tf_op jit(solution)/shard_map/concatenate | solution.py:683
  252.2 12.6 %reduce-scatter.4.cloned.1.call-done = bf16[1,192,768]{2,1,0:T(8,128)(2,1)} async-done(((bf16[16,192,768]{2,1,0:T(8,128)(2,1)}), bf16[1,192,768]{2,1,0:T(8,128)(2,1)}) %reduce-scatter.4.cloned.1.call-update) | async-done | bytes 294928 | tf_op jit(solution)/shard_map/reduce_scatter | solution.py:675
  264.8 114.4 %reduce-scatter.6.cloned.1.call-done = bf16[1,384,768]{2,1,0:T(8,128)(2,1)} async-done(((bf16[16,384,768]{2,1,0:T(8,128)(2,1)}), bf16[1,384,768]{2,1,0:T(8,128)(2,1)}) %reduce-scatter.6.cloned.1.call-update) | async-done | bytes 589840 | tf_op jit(solution)/shard_map/reduce_scatter | solution.py:675
  379.3 16.9 %tail.1 = (bf16[1176,768]{1,0:T(8,128)(2,1)}, bf16[1176,768]{1,0:T(8,128)(2,1)}) custom-call(bf16[3,1176,768]{2,1,0:T(8,128)(2,1)} %get-tuple-element.32.grad_ref, bf16[16,208,768]{2,1,0:T(8,128)(2,1)} %bitcast.21, bf16[16,208,768]{2,1,0:T(8,128)(2,1)} %bitcast.22, bf16[1176,768]{1,0:T(8,128)(2,1)} %token_ref.3, bf16[1176,768]{1,0:T(8,128)(2,1)} %cot_ref.7, ...), custom_call_target="tpu_custom_call" | custom-call | flops 5549064192 | bytes 21676032 | tf_op jit(solution)/shard_map/tail/pallas_call | solution.py:541
  396.2 43.4 %reduce-scatter.8.cloned.1.call-done = bf16[1,32,768]{2,1,0:T(8,128)(2,1)} async-done(((bf16[16,32,768]{2,1,0:T(8,128)(2,1)}), bf16[1,32,768]{2,1,0:T(8,128)(2,1)}) %reduce-scatter.8.cloned.1.call-update) | async-done | bytes 49168 | tf_op jit(solution)/shard_map/reduce_scatter | solution.py:675
  439.6 9.6 %psum.23 = bf16[32,768]{1,0:T(8,128)(2,1)S(1)} all-reduce(bf16[32,768]{1,0:T(8,128)(2,1)} %bitcast.25), channel_id=1, replica_groups=mesh['rep'=2,'fsdp'=16] {'rep'}, use_global_device_ids=true, to_apply=%region_7.8 | all-reduce | flops 24576 | bytes 98304 | tf_op jit(solution)/shard_map/psum | solution.py:678
  451.0 26.4 %all-reduce.5.cloned.1.call-done = (bf16[192,768]{1,0:T(8,128)(2,1)}, bf16[384,768]{1,0:T(8,128)(2,1)}) async-done(((bf16[192,768]{1,0:T(8,128)(2,1)}, bf16[384,768]{1,0:T(8,128)(2,1)}), (bf16[192,768]{1,0:T(8,128)(2,1)}, bf16[384,768]{1,0:T(8,128)(2,1)})) %all-reduce.5.cloned.1.call-update) | async-done | bytes 884752 | tf_op jit(solution)/shard_map/psum | solution.py:678
  477.4 1.2 convert_element_type.33
  478.6 1.8 slice.105
  480.4 1.0 convert_element_type.32
  (69 shorter events, 6.8 us)
Async XLA Ops:
  7.2 69.7 %all-gather.5.cloned.1.call-start = ((), (), s32[]{:S(2)}) async-start(), calls=%async_computation.6 | async-start | bytes 5431296 | tf_op jit(solution)/shard_map/all_gather | solution.py:637
  18.3 0.7 copy-start.5
  19.0 171.2 %all-gather.7.cloned.1.call-start = ((), (), s32[]{:S(2)}) async-start(), calls=%async_computation.7 | async-start | bytes 10027008 | tf_op jit(solution)/shard_map/all_gather | solution.py:642
  20.0 0.8 copy-start.3
  20.9 243.9 %reduce-scatter.4.cloned.1.call-start = ((), (), s32[]{:S(2)}) async-start(), calls=%async_computation.3 | async-start | bytes 5013504 | tf_op jit(solution)/shard_map/reduce_scatter | solution.py:675
  190.1 189.1 %reduce-scatter.6.cloned.1.call-start = ((), (), s32[]{:S(2)}) async-start(), calls=%async_computation.4 | async-start | bytes 10027008 | tf_op jit(solution)/shard_map/reduce_scatter | solution.py:675
  241.6 1.5 copy-start
  241.6 1.9 copy-start.7
  241.7 2.2 copy-start.6
  241.7 197.9 %reduce-scatter.8.cloned.1.call-start = ((), (), s32[]{:S(2)}) async-start(), calls=%async_computation.5 | async-start | bytes 835584 | tf_op jit(solution)/shard_map/reduce_scatter | solution.py:675
  252.1 225.3 %all-reduce.5.cloned.1.call-start = ((), (), s32[]{:S(2)}) async-start(), calls=%async_computation.8 | async-start | bytes 1769472 | tf_op jit(solution)/shard_map/psum | solution.py:678
  396.2 86.1 %copy-start.1 = (bf16[48,5376]{1,0:T(8,128)(2,1)S(1)}, bf16[48,5376]{1,0:T(8,128)(2,1)}, u32[]{:S(2)}) copy-start(bf16[48,5376]{1,0:T(8,128)(2,1)} %param.13) | copy-start | bytes 1548292
  477.4 4.0 copy-start.4
  477.4 5.1 %copy-start.8 = (bf16[48]{0:T(256)(128)(2,1)S(1)}, bf16[48]{0:T(256)(128)(2,1)}, u32[]{:S(2)}) copy-start(bf16[48]{0:T(256)(128)(2,1)} %param.16) | copy-start | bytes 292
  482.2 1.0 copy-start.2
Sparse Core Ops, SparseCore 0:
  19.1 57.7 all-gather.4
  79.8 79.4 all-gather.6
  190.2 74.5 reduce-scatter.3
  268.7 110.4 reduce-scatter.5
  383.2 56.3 reduce-scatter.7
  441.8 35.5 all-reduce.4
